TPU v7x, 256 devices: a whole 4x4x8 slice. The times are simulated.
256 devices in a mesh: rows: 128 (over x, z, y), cols: 2 (over core).
Axes of the slice: x: 4, y: 4, z: 8, core: 2. Of those that a mesh axis runs over, the one named last changes fastest.
Arguments:
- embeddings: bfloat16 [262144, 384], P('rows')
- test_matrix: bfloat16 [262144, 64], P('rows'), may hold values from -6 to 6
- pair_list: int32 [1024, 2], P(('rows', 'cols')), may hold values from -1 to 255, as said below
Outputs:
- orthonormal_basis: float32 [262144, 64], P(('rows', 'cols'))
- upper_factor: float32 [64, 64], replicated
Inputs may be any that keep to these rules, and one draw needn't show every extreme that they name: `pair_list`: device (r, c) holds 4 entries. Its live entries come first: pairs (i, j) with r * 2 <= i < (r + 1) * 2 and i <= j < min((r + 3) * 2, 256); each pair appears at most once over all devices; its other entries are -1 in both places. The device with c = 0 holds at least one live pair, the two devices of one r hold at most 4 together, and device (0, 0) holds exactly 4.
All inputs are finite; a program needn't handle non-finite values.
Results may differ from a plain program's by a relative error of at most 0.0053.
Values may be sent and summed in bfloat16 or wider, within the bound.
No kernel may reach another device: no remote copies, remote signals or barrier semaphores. Data moves between devices by JAX's collectives and lax.ppermute only.
A program may use at most 64 MiB of HBM per device.

v0:
```python
import jax
import jax.numpy as jnp
from jax import lax
from jax.sharding import PartitionSpec as P

BLK = 1024
SHARPNESS = 6.0
EPSILON = 1e-06


def shifted(value, axis, steps):
    count = lax.axis_size(axis)
    initial, last = (max(0, -steps), min(count, count - steps))
    return lax.ppermute(value, axis, [(source, source + steps) for source in range(initial, last)])


def unit_rows(embeddings):
    widened = embeddings.astype(jnp.float32)
    inverse = lax.rsqrt(jnp.sum(widened * widened, axis=1, keepdims=True) + EPSILON)
    return (widened * inverse).astype(jnp.bfloat16)


def affinity(left_rows, right_rows):
    scores = lax.dot_general(
        left_rows, right_rows, (((1,), (1,)), ((), ())), preferred_element_type=jnp.float32
    )
    return jnp.exp(SHARPNESS * (scores - 1.0)).astype(jnp.bfloat16)


def mirror_product(affinity_tile, vectors):
    return lax.dot_general(
        affinity_tile, vectors, (((0,), (0,)), ((), ())), preferred_element_type=jnp.float32
    )


def block_at(stacked, index):
    return lax.dynamic_index_in_dim(stacked, index, 0, keepdims=False)


def add_block(stacked, index, term):
    return lax.dynamic_update_index_in_dim(stacked, block_at(stacked, index) + term, index, 0)


def count_live(pair_rows):
    return jnp.sum((pair_rows[:, 0] >= 0).astype(jnp.int32))


def orthonormal(sketch_rows, rows_total):
    gram_matrix = lax.dot_general(
        sketch_rows,
        sketch_rows,
        (((0,), (0,)), ((), ())),
        precision=lax.Precision.HIGHEST,
        preferred_element_type=jnp.float32,
    )
    gram_matrix = lax.psum(gram_matrix, ("rows", "cols")) / rows_total
    lower_factor = jnp.linalg.cholesky(gram_matrix)
    solved = lax.linalg.triangular_solve(
        lower_factor, sketch_rows, left_side=False, lower=True, transpose_a=True
    )
    return (solved, lower_factor.T)


def affinity_pass(window_units, own_vectors, my_pairs, base_block):
    blocks_dev = own_vectors.shape[0]
    ahead_vectors = [shifted(own_vectors, "rows", -offset) for offset in (1, 2)]
    window_vectors = jnp.concatenate([own_vectors] + ahead_vectors, axis=0)
    initial = jnp.zeros(window_vectors.shape, jnp.float32)

    def pair_step(slot_index, accumulated):
        entry = my_pairs[slot_index]
        first_block = entry[0] - base_block
        second_block = entry[1] - base_block
        affinity_tile = affinity(
            block_at(window_units, first_block), block_at(window_units, second_block)
        )
        forward = jnp.dot(
            affinity_tile,
            block_at(window_vectors, second_block),
            preferred_element_type=jnp.float32,
        )
        accumulated = add_block(accumulated, first_block, forward)
        mirrored = first_block != second_block

        def add_mirror(current):
            return add_block(
                current,
                second_block,
                mirror_product(affinity_tile, block_at(window_vectors, first_block)),
            )

        return lax.cond(mirrored, add_mirror, lambda unchanged: unchanged, accumulated)

    accumulated = lax.fori_loop(0, count_live(my_pairs), pair_step, initial)
    own_blocks = accumulated[:blocks_dev]
    for offset in (1, 2):
        own_blocks = own_blocks + shifted(
            accumulated[offset * blocks_dev : (offset + 1) * blocks_dev], "rows", offset
        )
    flattened = own_blocks.reshape(-1, own_blocks.shape[2])
    return lax.psum_scatter(flattened, "cols", scatter_dimension=0, tiled=True)


def local(embeddings, test_matrix, pair_list):
    rows_dev = embeddings.shape[0]
    blocks_dev = rows_dev // BLK
    columns = test_matrix.shape[1]
    base_block = lax.axis_index("rows") * blocks_dev
    rows_total = rows_dev * lax.axis_size("rows")
    normed = unit_rows(embeddings).reshape(blocks_dev, BLK, embeddings.shape[1])
    ahead_units = [shifted(normed, "rows", -offset) for offset in (1, 2)]
    window_units = jnp.concatenate([normed] + ahead_units, axis=0)
    sketch_rows = affinity_pass(
        window_units, test_matrix.reshape(blocks_dev, BLK, columns), pair_list, base_block
    )
    panel_rows, _ = orthonormal(sketch_rows, rows_total)
    panel_whole = lax.all_gather(panel_rows.astype(jnp.bfloat16), "cols", axis=0, tiled=True)
    image_rows = affinity_pass(
        window_units, panel_whole.reshape(blocks_dev, BLK, columns), pair_list, base_block
    )
    return orthonormal(image_rows, rows_total)


def solution(mesh):
    in_specs = (P("rows", None), P("rows", None), P(("rows", "cols"), None))
    out_specs = (P(("rows", "cols"), None), P())
    return jax.shard_map(local, mesh=mesh, in_specs=in_specs, out_specs=out_specs, check_vma=False)
```

profile of v0, /device:TPU:1, one launch (start us, length us, event | category | flops | bytes accessed | tf_op | source)
XLA Modules:
  0.0 547.8 jit_solution(13680197383918252103)
XLA Ops:
  7.2 1.9 fusion.32
  15.7 85.9 %collective-permute-done.2 = bf16[2,1024,64]{2,1,0:T(8,128)(2,1)S(1)} collective-permute-done((bf16[2,1024,64]{2,1,0:T(8,128)(2,1)S(1)}, bf16[2,1024,64]{2,1,0:T(8,128)(2,1)S(1)}, u32[]{:S(2)}, u32[]{:S(2)}) %collective-permute-start.2) | collective-permute-done | bytes 262176 | tf_op jit(solution)/shard_map/ppermute | solution.py:14
  101.6 1.5 pad_maximum_fusion.1
  103.1 3.8 pad_maximum_fusion
  110.2 6.4 %collective-permute-start.4 = (f32[2,1024,64]{1,2,0:T(8,128)S(1)}, f32[2,1024,64]{1,2,0:T(8,128)S(1)}, u32[]{:S(2)}, u32[]{:S(2)}) collective-permute-start(f32[2,1024,64]{1,2,0:T(8,128)S(1)} %get-tuple-element.272), channel_id=1, source_target_pairs={{0,2},{2,4},{4,6},{6,8},{8,10},{10,12},{12,14},{14,16},{16,18},{18... | collective-permute-start | bytes 1572872 | tf_op jit(solution)/shard_map/ppermute | solution.py:14
  116.6 72.9 %collective-permute-start.5 = (f32[2,1024,64]{1,2,0:T(8,128)S(1)}, f32[2,1024,64]{1,2,0:T(8,128)S(1)}, u32[]{:S(2)}, u32[]{:S(2)}) collective-permute-start(f32[2,1024,64]{1,2,0:T(8,128)S(1)} %get-tuple-element.273), channel_id=1, source_target_pairs={{0,4},{2,6},{4,8},{6,10},{8,12},{10,14},{12,16},{14,18},{16,20},{1... | collective-permute-start | bytes 1572872 | tf_op jit(solution)/shard_map/ppermute | solution.py:14
  189.5 6.1 %collective-permute-done.5 = f32[2,1024,64]{1,2,0:T(8,128)S(1)} collective-permute-done((f32[2,1024,64]{1,2,0:T(8,128)S(1)}, f32[2,1024,64]{1,2,0:T(8,128)S(1)}, u32[]{:S(2)}, u32[]{:S(2)}) %collective-permute-start.5) | collective-permute-done | bytes 524320 | tf_op jit(solution)/shard_map/ppermute | solution.py:14
  197.7 36.3 %reduce-scatter.3.cloned.1.call-done = f32[1024,64]{0,1:T(8,128)} async-done(((f32[2048,64]{0,1:T(8,128)}), f32[1024,64]{0,1:T(8,128)}) %reduce-scatter.3.cloned.1.call-update) | async-done | bytes 262160 | tf_op jit(solution)/shard_map/reduce_scatter | solution.py:101
  234.0 1.4 fusion.49
  235.5 77.5 %psum.14 = f32[64,64]{0,1:T(8,128)S(1)} all-reduce(f32[64,64]{0,1:T(8,128)S(1)} %fusion.49), channel_id=1, replica_groups=mesh['rows'=128,'cols'=2] {'rows','cols'}, use_global_device_ids=true, to_apply=%region_7.8 | all-reduce | flops 4096 | bytes 32768 | tf_op jit(solution)/shard_map/psum | solution.py:56
  313.1 5.8 %cholesky.44 = f32[64,64]{1,0:T(8,128)S(1)} custom-call(f32[64,64]{1,0:T(8,128)S(1)} %fusion.39), custom_call_target="Cholesky" | custom-call | tf_op jit(solution)/shard_map/jit(cholesky)/cholesky | solution.py:57
  320.3 4.9 custom-call.6
  326.6 2.5 all_gather.3
  332.0 22.3 %collective-permute-done.6 = bf16[2,1024,64]{2,1,0:T(8,128)(2,1)S(1)} collective-permute-done((bf16[2,1024,64]{2,1,0:T(8,128)(2,1)S(1)}, bf16[2,1024,64]{2,1,0:T(8,128)(2,1)S(1)}, u32[]{:S(2)}, u32[]{:S(2)}) %collective-permute-start.6) | collective-permute-done | bytes 262176 | tf_op jit(solution)/shard_map/ppermute | solution.py:14
  354.2 1.5 pad_maximum_fusion.2
  359.1 3.7 collective-permute-start.8
  362.7 45.1 %collective-permute-start.9 = (f32[2,1024,64]{1,2,0:T(8,128)S(1)}, f32[2,1024,64]{1,2,0:T(8,128)S(1)}, u32[]{:S(2)}, u32[]{:S(2)}) collective-permute-start(f32[2,1024,64]{1,2,0:T(8,128)S(1)} %get-tuple-element.271), channel_id=1, source_target_pairs={{0,4},{2,6},{4,8},{6,10},{8,12},{10,14},{12,16},{14,18},{16,20},{1... | collective-permute-start | bytes 1572872 | tf_op jit(solution)/shard_map/ppermute | solution.py:14
  407.8 11.5 %collective-permute-done.9 = f32[2,1024,64]{1,2,0:T(8,128)S(1)} collective-permute-done((f32[2,1024,64]{1,2,0:T(8,128)S(1)}, f32[2,1024,64]{1,2,0:T(8,128)S(1)}, u32[]{:S(2)}, u32[]{:S(2)}) %collective-permute-start.9) | collective-permute-done | bytes 524320 | tf_op jit(solution)/shard_map/ppermute | solution.py:14
  421.3 25.8 %reduce-scatter.5.cloned.1.call-done = f32[1024,64]{0,1:T(8,128)} async-done(((f32[2048,64]{0,1:T(8,128)}), f32[1024,64]{0,1:T(8,128)}) %reduce-scatter.5.cloned.1.call-update) | async-done | bytes 262160 | tf_op jit(solution)/shard_map/reduce_scatter | solution.py:101
  447.1 1.4 fusion.50
  448.4 77.5 %psum.15 = f32[64,64]{0,1:T(8,128)S(1)} all-reduce(f32[64,64]{0,1:T(8,128)S(1)} %fusion.50), channel_id=1, replica_groups=mesh['rows'=128,'cols'=2] {'rows','cols'}, use_global_device_ids=true, to_apply=%region_15.18 | all-reduce | flops 4096 | bytes 32768 | tf_op jit(solution)/shard_map/psum | solution.py:56
  526.1 5.8 %cholesky.55 = f32[64,64]{1,0:T(8,128)S(1)} custom-call(f32[64,64]{1,0:T(8,128)S(1)} %fusion.37), custom_call_target="Cholesky" | custom-call | tf_op jit(solution)/shard_map/jit(cholesky)/cholesky | solution.py:57
  533.3 4.9 custom-call.7
  538.9 2.1 convolution_bitcast_fusion.2
  (51 shorter events, 24.9 us)
Async XLA Ops:
  7.2 2.0 copy-start
  7.2 226.9 %reduce-scatter.3.cloned.1.call-start = ((), (), s32[]{:S(2)}) async-start(), calls=%async_computation.2 | async-start | bytes 786432 | tf_op jit(solution)/shard_map/reduce_scatter | solution.py:101
  9.1 3.0 copy-start.1
  9.2 5.9 %copy-start.2 = (s32[4,2]{0,1:T(2,128)S(1)}, s32[4,2]{0,1:T(2,128)}, u32[]{:S(2)}) copy-start(s32[4,2]{0,1:T(2,128)} %param.16) | copy-start | bytes 100
  9.5 93.6 %collective-permute-start = (bf16[2,1024,384]{2,1,0:T(8,128)(2,1)S(1)}, bf16[2,1024,384]{2,1,0:T(8,128)(2,1)}, u32[]{:S(2)}, u32[]{:S(2)}) collective-permute-start(bf16[2,1024,384]{2,1,0:T(8,128)(2,1)S(1)} %bitcast.145), channel_id=1, source_target_pairs={{2,0},{4,2},{6,4},{8,6},{10,8},{12,10},{14,12},{16,14},{18,16},{20... | collective-permute-start | bytes 4718600 | tf_op jit(solution)/shard_map/ppermute | solution.py:14
  10.8 92.3 %collective-permute-start.1 = (bf16[2,1024,384]{2,1,0:T(8,128)(2,1)S(1)}, bf16[2,1024,384]{2,1,0:T(8,128)(2,1)}, u32[]{:S(2)}, u32[]{:S(2)}) collective-permute-start(bf16[2,1024,384]{2,1,0:T(8,128)(2,1)S(1)} %bitcast.146), channel_id=1, source_target_pairs={{4,0},{6,2},{8,4},{10,6},{12,8},{14,10},{16,12},{18,14},{20,16},{2... | collective-permute-start | bytes 4718600 | tf_op jit(solution)/shard_map/ppermute | solution.py:14
  12.4 89.2 %collective-permute-start.2 = (bf16[2,1024,64]{2,1,0:T(8,128)(2,1)S(1)}, bf16[2,1024,64]{2,1,0:T(8,128)(2,1)S(1)}, u32[]{:S(2)}, u32[]{:S(2)}) collective-permute-start(bf16[2,1024,64]{2,1,0:T(8,128)(2,1)S(1)} %bitcast.150), channel_id=1, source_target_pairs={{2,0},{4,2},{6,4},{8,6},{10,8},{12,10},{14,12},{16,14},{18,16},{20... | collective-permute-start | bytes 786440 | tf_op jit(solution)/shard_map/ppermute | solution.py:14
  13.7 87.9 %collective-permute-start.3 = (bf16[2,1024,64]{2,1,0:T(8,128)(2,1)S(1)}, bf16[2,1024,64]{2,1,0:T(8,128)(2,1)S(1)}, u32[]{:S(2)}, u32[]{:S(2)}) collective-permute-start(bf16[2,1024,64]{2,1,0:T(8,128)(2,1)S(1)} %bitcast.151), channel_id=1, source_target_pairs={{4,0},{6,2},{8,4},{10,6},{12,8},{14,10},{16,12},{18,14},{20,16},{2... | collective-permute-start | bytes 786440 | tf_op jit(solution)/shard_map/ppermute | solution.py:14
  110.2 79.3 %collective-permute-start.4 = (f32[2,1024,64]{1,2,0:T(8,128)S(1)}, f32[2,1024,64]{1,2,0:T(8,128)S(1)}, u32[]{:S(2)}, u32[]{:S(2)}) collective-permute-start(f32[2,1024,64]{1,2,0:T(8,128)S(1)} %get-tuple-element.272), channel_id=1, source_target_pairs={{0,2},{2,4},{4,6},{6,8},{8,10},{10,12},{12,14},{14,16},{16,18},{18... | collective-permute-start | bytes 1572872 | tf_op jit(solution)/shard_map/ppermute | solution.py:14
  116.6 79.0 %collective-permute-start.5 = (f32[2,1024,64]{1,2,0:T(8,128)S(1)}, f32[2,1024,64]{1,2,0:T(8,128)S(1)}, u32[]{:S(2)}, u32[]{:S(2)}) collective-permute-start(f32[2,1024,64]{1,2,0:T(8,128)S(1)} %get-tuple-element.273), channel_id=1, source_target_pairs={{0,4},{2,6},{4,8},{6,10},{8,12},{10,14},{12,16},{14,18},{16,20},{1... | collective-permute-start | bytes 1572872 | tf_op jit(solution)/shard_map/ppermute | solution.py:14
  197.7 249.4 %reduce-scatter.5.cloned.1.call-start = ((), (), s32[]{:S(2)}) async-start(), calls=%async_computation.3 | async-start | bytes 786432 | tf_op jit(solution)/shard_map/reduce_scatter | solution.py:101
  329.4 24.9 %collective-permute-start.6 = (bf16[2,1024,64]{2,1,0:T(8,128)(2,1)S(1)}, bf16[2,1024,64]{2,1,0:T(8,128)(2,1)S(1)}, u32[]{:S(2)}, u32[]{:S(2)}) collective-permute-start(bf16[2,1024,64]{2,1,0:T(8,128)(2,1)S(1)} %bitcast.153), channel_id=1, source_target_pairs={{2,0},{4,2},{6,4},{8,6},{10,8},{12,10},{14,12},{16,14},{18,16},{20... | collective-permute-start | bytes 786440 | tf_op jit(solution)/shard_map/ppermute | solution.py:14
  330.7 23.6 %collective-permute-start.7 = (bf16[2,1024,64]{2,1,0:T(8,128)(2,1)S(1)}, bf16[2,1024,64]{2,1,0:T(8,128)(2,1)S(1)}, u32[]{:S(2)}, u32[]{:S(2)}) collective-permute-start(bf16[2,1024,64]{2,1,0:T(8,128)(2,1)S(1)} %bitcast.154), channel_id=1, source_target_pairs={{4,0},{6,2},{8,4},{10,6},{12,8},{14,10},{16,12},{18,14},{20,16},{2... | collective-permute-start | bytes 786440 | tf_op jit(solution)/shard_map/ppermute | solution.py:14
  359.1 48.8 %collective-permute-start.8 = (f32[2,1024,64]{1,2,0:T(8,128)S(1)}, f32[2,1024,64]{1,2,0:T(8,128)S(1)}, u32[]{:S(2)}, u32[]{:S(2)}) collective-permute-start(f32[2,1024,64]{1,2,0:T(8,128)S(1)} %get-tuple-element.270), channel_id=1, source_target_pairs={{0,2},{2,4},{4,6},{6,8},{8,10},{10,12},{12,14},{14,16},{16,18},{18... | collective-permute-start | bytes 1572872 | tf_op jit(solution)/shard_map/ppermute | solution.py:14
  362.7 56.6 %collective-permute-start.9 = (f32[2,1024,64]{1,2,0:T(8,128)S(1)}, f32[2,1024,64]{1,2,0:T(8,128)S(1)}, u32[]{:S(2)}, u32[]{:S(2)}) collective-permute-start(f32[2,1024,64]{1,2,0:T(8,128)S(1)} %get-tuple-element.271), channel_id=1, source_target_pairs={{0,4},{2,6},{4,8},{6,10},{8,12},{10,14},{12,16},{14,18},{16,20},{1... | collective-permute-start | bytes 1572872 | tf_op jit(solution)/shard_map/ppermute | solution.py:14
Sparse Core Ops, SparseCore 0:
  197.8 36.2 reduce-scatter.2
  421.4 25.5 reduce-scatter.4
where the time goes:
time: 550 us; the launch traced here: 548 us
  waiting for transfers between devices  188 us (34%)
  blocking collectives  158 us (29%)
  starting transfers between devices  136 us (25%)
  other arithmetic  36.2 us (7%)
  between operations  14.3 us (3%)
  local copies, waits for them, and re-layouts  8.38 us (2%)
  matrix products  6.27 us (1%)
    psum x2, blocking collectives, orthonormal(): gram_matrix = lax.psum(gram_matrix, ('rows', 'cols')) / rows_total  155 us
    ppermute x10, starting transfers between devices, shifted(): lax.ppermute(value, axis, [(source, source + steps) for source in range(i...  136 us
    ppermute x10, waiting for transfers between devices, shifted(): lax.ppermute(value, axis, [(source, source + steps) for source in range(i...  126 us
    reduce_scatter x2, waiting for transfers between devices, affinity_pass(): return lax.psum_scatter(flattened, 'cols', scatter_dimension=0, tiled=True)  62.1 us
    another operation x6, other arithmetic, orthonormal(): lower_factor = jnp.linalg.cholesky(gram_matrix)  13 us
  transfers between devices with their start and end apart: 12, of which 6 were waited for; matrix products, arithmetic and copies ran while one was open for 0% of the time, Pallas kernels for 0%

commit v1 on v0

--- a/solution.py
+++ b/solution.py
@@ -53,7 +53,7 @@
         precision=lax.Precision.HIGHEST,
         preferred_element_type=jnp.float32,
     )
-    gram_matrix = lax.psum(gram_matrix, ("rows", "cols")) / rows_total
+    gram_matrix = lax.psum(lax.psum(gram_matrix, "rows"), "cols") / rows_total
     lower_factor = jnp.linalg.cholesky(gram_matrix)
     solved = lax.linalg.triangular_solve(
         lower_factor, sketch_rows, left_side=False, lower=True, transpose_a=True

time: 550 us -> 1760 us (3.20)
  blocking collectives: 158 us -> 1390 us
  starting transfers between devices: 136 us -> 117 us
    psum x2 -> x4, blocking collectives: 155 us -> 1380 us  [orthonormal(): gram_matrix = lax.psum(lax.psum(gram_matrix, 'rows'), 'cols') / rows_total]
    ppermute x10, starting transfers between devices: 136 us -> 117 us  [shifted(): lax.ppermute(value, axis, [(source, source + steps) for source in range(i...]
where the time goes in v1:
time: 1760 us
  blocking collectives  1390 us (79%)
  waiting for transfers between devices  187 us (11%)
  starting transfers between devices  117 us (7%)
  other arithmetic  36.2 us (2%)
    psum x4, blocking collectives, orthonormal(): gram_matrix = lax.psum(lax.psum(gram_matrix, 'rows'), 'cols') / rows_total  1380 us
    ppermute x10, waiting for transfers between devices, shifted(): lax.ppermute(value, axis, [(source, source + steps) for source in range(i...  121 us
    ppermute x10, starting transfers between devices, shifted(): lax.ppermute(value, axis, [(source, source + steps) for source in range(i...  117 us
    reduce_scatter x2, waiting for transfers between devices, affinity_pass(): return lax.psum_scatter(flattened, 'cols', scatter_dimension=0, tiled=True)  66.1 us
  transfers between devices with their start and end apart: 12, of which 6 were waited for; matrix products, arithmetic and copies ran while one was open for 0% of the time, Pallas kernels for 0%

profile of v1, /device:TPU:1, one launch (start us, length us, event | category | flops | bytes accessed | tf_op | source)
XLA Modules:
  0.0 1757.5 jit_solution(5639679917790080270)
XLA Ops:
  7.2 1.9 fusion.32
  15.7 85.9 %collective-permute-done.2 = bf16[2,1024,64]{2,1,0:T(8,128)(2,1)S(1)} collective-permute-done((bf16[2,1024,64]{2,1,0:T(8,128)(2,1)S(1)}, bf16[2,1024,64]{2,1,0:T(8,128)(2,1)S(1)}, u32[]{:S(2)}, u32[]{:S(2)}) %collective-permute-start.2) | collective-permute-done | bytes 262176 | tf_op jit(solution)/shard_map/ppermute | solution.py:14
  101.6 1.5 pad_maximum_fusion.1
  103.1 3.8 pad_maximum_fusion
  110.2 6.4 collective-permute-start.4
  116.6 72.6 %collective-permute-start.5 = (f32[2,1024,64]{1,2,0:T(8,128)S(1)}, f32[2,1024,64]{1,2,0:T(8,128)S(1)}, u32[]{:S(2)}, u32[]{:S(2)}) collective-permute-start(f32[2,1024,64]{1,2,0:T(8,128)S(1)} %get-tuple-element.273), channel_id=1, source_target_pairs={{0,4},{2,6},{4,8},{6,10},{8,12},{10,14},{12,16},{14,18},{16,20},{1... | collective-permute-start | bytes 1572872 | tf_op jit(solution)/shard_map/ppermute | solution.py:14
  189.2 6.1 collective-permute-done.5
  197.4 36.3 %reduce-scatter.3.cloned.1.call-done = f32[1024,64]{0,1:T(8,128)} async-done(((f32[2048,64]{0,1:T(8,128)}), f32[1024,64]{0,1:T(8,128)}) %reduce-scatter.3.cloned.1.call-update) | async-done | bytes 262160 | tf_op jit(solution)/shard_map/reduce_scatter | solution.py:101
  233.7 1.4 fusion.49
  235.1 579.0 %psum.28 = f32[64,64]{0,1:T(8,128)S(1)} all-reduce(f32[64,64]{0,1:T(8,128)S(1)} %fusion.49), channel_id=1, replica_groups=mesh['rows'=128,'cols'=2] {'rows'}, use_global_device_ids=true, to_apply=%region_7.8 | all-reduce | flops 4096 | bytes 32768 | tf_op jit(solution)/shard_map/psum | solution.py:56
  814.1 113.3 %psum.29 = f32[64,64]{0,1:T(8,128)S(1)} all-reduce(f32[64,64]{0,1:T(8,128)S(1)} %psum.28), channel_id=1, replica_groups=mesh['rows'=128,'cols'=2] {'cols'}, use_global_device_ids=true, to_apply=%region_8.9 | all-reduce | flops 4096 | bytes 32768 | tf_op jit(solution)/shard_map/psum | solution.py:56
  927.5 5.8 cholesky.44
  934.7 4.9 custom-call.6
  941.0 2.0 all_gather.3
  945.9 22.9 %collective-permute-done.6 = bf16[2,1024,64]{2,1,0:T(8,128)(2,1)S(1)} collective-permute-done((bf16[2,1024,64]{2,1,0:T(8,128)(2,1)S(1)}, bf16[2,1024,64]{2,1,0:T(8,128)(2,1)S(1)}, u32[]{:S(2)}, u32[]{:S(2)}) %collective-permute-start.6) | collective-permute-done | bytes 262176 | tf_op jit(solution)/shard_map/ppermute | solution.py:14
  968.8 1.5 pad_maximum_fusion.2
  975.0 29.1 %collective-permute-start.9 = (f32[2,1024,64]{1,2,0:T(8,128)S(1)}, f32[2,1024,64]{1,2,0:T(8,128)S(1)}, u32[]{:S(2)}, u32[]{:S(2)}) collective-permute-start(f32[2,1024,64]{1,2,0:T(8,128)S(1)} %get-tuple-element.271), channel_id=1, source_target_pairs={{0,4},{2,6},{4,8},{6,10},{8,12},{10,14},{12,16},{14,18},{16,20},{1... | collective-permute-start | bytes 1572872 | tf_op jit(solution)/shard_map/ppermute | solution.py:14
  1004.0 6.1 collective-permute-done.9
  1012.2 29.8 %reduce-scatter.5.cloned.1.call-done = f32[1024,64]{0,1:T(8,128)} async-done(((f32[2048,64]{0,1:T(8,128)}), f32[1024,64]{0,1:T(8,128)}) %reduce-scatter.5.cloned.1.call-update) | async-done | bytes 262160 | tf_op jit(solution)/shard_map/reduce_scatter | solution.py:101
  1043.4 579.0 %psum.30 = f32[64,64]{0,1:T(8,128)S(1)} all-reduce(f32[64,64]{0,1:T(8,128)S(1)} %fusion.50), channel_id=1, replica_groups=mesh['rows'=128,'cols'=2] {'rows'}, use_global_device_ids=true, to_apply=%region_16.19 | all-reduce | flops 4096 | bytes 32768 | tf_op jit(solution)/shard_map/psum | solution.py:56
  1622.4 113.3 %psum.31 = f32[64,64]{0,1:T(8,128)S(1)} all-reduce(f32[64,64]{0,1:T(8,128)S(1)} %psum.30), channel_id=1, replica_groups=mesh['rows'=128,'cols'=2] {'cols'}, use_global_device_ids=true, to_apply=%region_17.20 | all-reduce | flops 4096 | bytes 32768 | tf_op jit(solution)/shard_map/psum | solution.py:56
  1735.8 5.8 cholesky.55
  1743.0 4.9 custom-call.7
  1748.6 2.1 convolution_bitcast_fusion.2
  (53 shorter events, 27.6 us)
Async XLA Ops:
  7.2 2.0 copy-start
  7.2 226.5 %reduce-scatter.3.cloned.1.call-start = ((), (), s32[]{:S(2)}) async-start(), calls=%async_computation.2 | async-start | bytes 786432 | tf_op jit(solution)/shard_map/reduce_scatter | solution.py:101
  9.1 3.0 copy-start.1
  9.2 5.9 copy-start.2
  9.5 93.6 %collective-permute-start = (bf16[2,1024,384]{2,1,0:T(8,128)(2,1)S(1)}, bf16[2,1024,384]{2,1,0:T(8,128)(2,1)}, u32[]{:S(2)}, u32[]{:S(2)}) collective-permute-start(bf16[2,1024,384]{2,1,0:T(8,128)(2,1)S(1)} %bitcast.145), channel_id=1, source_target_pairs={{2,0},{4,2},{6,4},{8,6},{10,8},{12,10},{14,12},{16,14},{18,16},{20... | collective-permute-start | bytes 4718600 | tf_op jit(solution)/shard_map/ppermute | solution.py:14
  10.8 92.3 %collective-permute-start.1 = (bf16[2,1024,384]{2,1,0:T(8,128)(2,1)S(1)}, bf16[2,1024,384]{2,1,0:T(8,128)(2,1)}, u32[]{:S(2)}, u32[]{:S(2)}) collective-permute-start(bf16[2,1024,384]{2,1,0:T(8,128)(2,1)S(1)} %bitcast.146), channel_id=1, source_target_pairs={{4,0},{6,2},{8,4},{10,6},{12,8},{14,10},{16,12},{18,14},{20,16},{2... | collective-permute-start | bytes 4718600 | tf_op jit(solution)/shard_map/ppermute | solution.py:14
  12.4 89.2 %collective-permute-start.2 = (bf16[2,1024,64]{2,1,0:T(8,128)(2,1)S(1)}, bf16[2,1024,64]{2,1,0:T(8,128)(2,1)S(1)}, u32[]{:S(2)}, u32[]{:S(2)}) collective-permute-start(bf16[2,1024,64]{2,1,0:T(8,128)(2,1)S(1)} %bitcast.150), channel_id=1, source_target_pairs={{2,0},{4,2},{6,4},{8,6},{10,8},{12,10},{14,12},{16,14},{18,16},{20... | collective-permute-start | bytes 786440 | tf_op jit(solution)/shard_map/ppermute | solution.py:14
  13.7 87.9 %collective-permute-start.3 = (bf16[2,1024,64]{2,1,0:T(8,128)(2,1)S(1)}, bf16[2,1024,64]{2,1,0:T(8,128)(2,1)S(1)}, u32[]{:S(2)}, u32[]{:S(2)}) collective-permute-start(bf16[2,1024,64]{2,1,0:T(8,128)(2,1)S(1)} %bitcast.151), channel_id=1, source_target_pairs={{4,0},{6,2},{8,4},{10,6},{12,8},{14,10},{16,12},{18,14},{20,16},{2... | collective-permute-start | bytes 786440 | tf_op jit(solution)/shard_map/ppermute | solution.py:14
  110.2 79.0 %collective-permute-start.4 = (f32[2,1024,64]{1,2,0:T(8,128)S(1)}, f32[2,1024,64]{1,2,0:T(8,128)S(1)}, u32[]{:S(2)}, u32[]{:S(2)}) collective-permute-start(f32[2,1024,64]{1,2,0:T(8,128)S(1)} %get-tuple-element.272), channel_id=1, source_target_pairs={{0,2},{2,4},{4,6},{6,8},{8,10},{10,12},{12,14},{14,16},{16,18},{18... | collective-permute-start | bytes 1572872 | tf_op jit(solution)/shard_map/ppermute | solution.py:14
  116.6 78.7 %collective-permute-start.5 = (f32[2,1024,64]{1,2,0:T(8,128)S(1)}, f32[2,1024,64]{1,2,0:T(8,128)S(1)}, u32[]{:S(2)}, u32[]{:S(2)}) collective-permute-start(f32[2,1024,64]{1,2,0:T(8,128)S(1)} %get-tuple-element.273), channel_id=1, source_target_pairs={{0,4},{2,6},{4,8},{6,10},{8,12},{10,14},{12,16},{14,18},{16,20},{1... | collective-permute-start | bytes 1572872 | tf_op jit(solution)/shard_map/ppermute | solution.py:14
  197.4 844.6 %reduce-scatter.5.cloned.1.call-start = ((), (), s32[]{:S(2)}) async-start(), calls=%async_computation.3 | async-start | bytes 786432 | tf_op jit(solution)/shard_map/reduce_scatter | solution.py:101
  943.3 25.5 %collective-permute-start.6 = (bf16[2,1024,64]{2,1,0:T(8,128)(2,1)S(1)}, bf16[2,1024,64]{2,1,0:T(8,128)(2,1)S(1)}, u32[]{:S(2)}, u32[]{:S(2)}) collective-permute-start(bf16[2,1024,64]{2,1,0:T(8,128)(2,1)S(1)} %bitcast.153), channel_id=1, source_target_pairs={{2,0},{4,2},{6,4},{8,6},{10,8},{12,10},{14,12},{16,14},{18,16},{20... | collective-permute-start | bytes 786440 | tf_op jit(solution)/shard_map/ppermute | solution.py:14
  944.6 24.2 %collective-permute-start.7 = (bf16[2,1024,64]{2,1,0:T(8,128)(2,1)S(1)}, bf16[2,1024,64]{2,1,0:T(8,128)(2,1)S(1)}, u32[]{:S(2)}, u32[]{:S(2)}) collective-permute-start(bf16[2,1024,64]{2,1,0:T(8,128)(2,1)S(1)} %bitcast.154), channel_id=1, source_target_pairs={{4,0},{6,2},{8,4},{10,6},{12,8},{14,10},{16,12},{18,14},{20,16},{2... | collective-permute-start | bytes 786440 | tf_op jit(solution)/shard_map/ppermute | solution.py:14
  973.6 30.4 %collective-permute-start.8 = (f32[2,1024,64]{1,2,0:T(8,128)S(1)}, f32[2,1024,64]{1,2,0:T(8,128)S(1)}, u32[]{:S(2)}, u32[]{:S(2)}) collective-permute-start(f32[2,1024,64]{1,2,0:T(8,128)S(1)} %get-tuple-element.270), channel_id=1, source_target_pairs={{0,2},{2,4},{4,6},{6,8},{8,10},{10,12},{12,14},{14,16},{16,18},{18... | collective-permute-start | bytes 1572872 | tf_op jit(solution)/shard_map/ppermute | solution.py:14
  975.0 35.2 %collective-permute-start.9 = (f32[2,1024,64]{1,2,0:T(8,128)S(1)}, f32[2,1024,64]{1,2,0:T(8,128)S(1)}, u32[]{:S(2)}, u32[]{:S(2)}) collective-permute-start(f32[2,1024,64]{1,2,0:T(8,128)S(1)} %get-tuple-element.271), channel_id=1, source_target_pairs={{0,4},{2,6},{4,8},{6,10},{8,12},{10,14},{12,16},{14,18},{16,20},{1... | collective-permute-start | bytes 1572872 | tf_op jit(solution)/shard_map/ppermute | solution.py:14
Sparse Core Ops, SparseCore 0:
  197.5 36.1 reduce-scatter.2
  1012.3 29.6 reduce-scatter.4
